TPU v7x, 32 devices: a whole 2x2x4 slice. The times are simulated.
32 devices in a mesh: dp: 8 (over z, core), fsdp: 4 (over y, x).
Axes of the slice: x: 2, y: 2, z: 4, core: 2. Of those that a mesh axis runs over, the one named last changes fastest.
Arguments:
- inputs: bfloat16 [64, 512, 768], P(('dp', 'fsdp')), may hold values from -6 to 6
- segment_ids: int32 [64, 512], P(('dp', 'fsdp')), may hold values from 0 to 3, never falling along the last dimension, each value on 1 to 256 neighbouring positions
- cotangent: bfloat16 [64, 512, 768], P(('dp', 'fsdp')), may hold values from -9 to 9
- qkv_weight: bfloat16 [768, 2304], P(('dp', 'fsdp')), may hold values from -0.21875 to 0.21875
- out_weight: bfloat16 [768, 768], P(('dp', 'fsdp')), may hold values from -1.75 to 1.75
- up_weight: bfloat16 [768, 3072], P(('dp', 'fsdp')), may hold values from -0.21875 to 0.21875
- down_weight: bfloat16 [3072, 768], P(('dp', 'fsdp')), may hold values from -0.109375 to 0.109375
- query_bias_vector: bfloat16 [768], P(('dp', 'fsdp')), may hold values from -1.5 to 1.5
- value_bias_vector: bfloat16 [768], P(('dp', 'fsdp')), may hold values from -1.5 to 1.5
- out_bias: bfloat16 [768], P(('dp', 'fsdp')), may hold values from -1.5 to 1.5
- gain_one: bfloat16 [768], P(('dp', 'fsdp')), may hold values from 0.5 to 1.5
- shift_one: bfloat16 [768], P(('dp', 'fsdp')), may hold values from -1.5 to 1.5
- up_bias: bfloat16 [3072], P(('dp', 'fsdp')), may hold values from -1.5 to 1.5
- down_bias: bfloat16 [768], P(('dp', 'fsdp')), may hold values from -1.5 to 1.5
- gain_two: bfloat16 [768], P(('dp', 'fsdp')), may hold values from 0.5 to 1.5
- shift_two: bfloat16 [768], P(('dp', 'fsdp')), may hold values from -1.5 to 1.5
- query_down: bfloat16 [768, 8], replicated, may hold values from -0.21875 to 0.21875
- query_up_weight: bfloat16 [8, 768], replicated, may hold values from -2 to 2
- value_down: bfloat16 [768, 8], replicated, may hold values from -0.21875 to 0.21875
- value_up_weight: bfloat16 [8, 768], replicated, may hold values from -2 to 2
Outputs:
- output: bfloat16 [64, 512, 768], P(('dp', 'fsdp'))
- grad_input: float32 [64, 512, 768], P(('dp', 'fsdp'))
- grad_query_down: float32 [768, 8], replicated
- grad_query_up: float32 [8, 768], replicated
- grad_value_down: float32 [768, 8], replicated
- grad_value_up: float32 [8, 768], replicated
Inputs may be any that keep to these rules, and one draw needn't show every extreme that they name: `segment_ids`: within a pack the ids never fall; each of the 4 documents has 1 to 256 rows, and one has exactly 256.
All inputs are finite; a program needn't handle non-finite values.
Results may differ from a plain program's by a relative error of at most 0.015.
The roundings to bfloat16 on the way count: a program that leaves them out, or rounds other values in their place, can miss the bound.
Values may be sent and summed in bfloat16 or wider, within the bound.
No kernel may reach another device: no remote copies, remote signals or barrier semaphores. Data moves between devices by JAX's collectives and lax.ppermute only.
A program may use at most 128 MiB of HBM per device.

v0:
```python
from functools import partial
import jax
import jax.numpy as jnp
from jax import lax
from jax.sharding import PartitionSpec as P

HEADS = 12
HEAD_DIM = 64
highest_precision_mode = lax.Precision.HIGHEST
norm_epsilon = 1e-05
adapter_scale = 2.0


def layer_norm(value_rows, gain, shift):
    centred = value_rows - jnp.mean(value_rows, axis=-1, keepdims=True)
    variance = jnp.mean(centred * centred, axis=-1, keepdims=True)
    return centred * lax.rsqrt(variance + norm_epsilon) * gain + shift


def gelu_exact(value_rows):
    return jax.nn.gelu(value_rows, approximate=False)


def fetch_forward(qkv_weight, out_weight, up_weight, down_weight, vectors, up_bias):
    return (
        lax.all_gather(qkv_weight, ("dp", "fsdp"), axis=0, tiled=True),
        lax.all_gather(out_weight, ("dp", "fsdp"), axis=0, tiled=True),
        lax.all_gather(up_weight, ("dp", "fsdp"), axis=0, tiled=True),
        lax.all_gather(down_weight, ("dp", "fsdp"), axis=0, tiled=True),
        lax.all_gather(vectors, ("dp", "fsdp"), axis=1, tiled=True),
        lax.all_gather(up_bias, ("dp", "fsdp"), axis=0, tiled=True),
    )


def fetch_backward(qkv_weight, out_weight, up_weight, down_weight, gains):
    return (
        lax.all_gather(qkv_weight, ("dp", "fsdp"), axis=0, tiled=True),
        lax.all_gather(out_weight, ("dp", "fsdp"), axis=0, tiled=True),
        lax.all_gather(up_weight, ("dp", "fsdp"), axis=0, tiled=True),
        lax.all_gather(down_weight, ("dp", "fsdp"), axis=0, tiled=True),
        lax.all_gather(gains, ("dp", "fsdp"), axis=1, tiled=True),
    )


def segment_mask(segment):
    return (segment[:, None] == segment[None, :])[None]


def attend_pack(packed):
    query_rows, key_rows, value_rows, segment = packed
    scale = query_rows.shape[-1] ** (-0.5)
    raw_scores = jnp.einsum(
        "qhd,khd->hqk", query_rows, key_rows, preferred_element_type=jnp.float32
    )
    in_segment = segment_mask(segment)
    masked = jnp.where(in_segment, raw_scores * scale, -jnp.inf)
    highest = jnp.max(masked, axis=-1, keepdims=True)
    exponent = jnp.where(in_segment, jnp.exp(masked - highest), 0.0)
    row_total = jnp.sum(exponent, axis=-1, keepdims=True)
    probs_low = (exponent / row_total).astype(jnp.bfloat16)
    attended = jnp.einsum("hqk,khd->qhd", probs_low, value_rows, preferred_element_type=jnp.float32)
    return (attended, (highest + jnp.log(row_total))[..., 0])


def attend_back(packed):
    query_rows, key_rows, value_rows, segment, log_total, grad_mixed = packed
    scale = query_rows.shape[-1] ** (-0.5)
    raw_scores = jnp.einsum(
        "qhd,khd->hqk", query_rows, key_rows, preferred_element_type=jnp.float32
    )
    in_segment = segment_mask(segment)
    probs = jnp.where(in_segment, jnp.exp(raw_scores * scale - log_total[..., None]), 0.0)
    value_rows_gradient = jnp.einsum(
        "hqk,qhd->khd", probs.astype(jnp.bfloat16), grad_mixed, preferred_element_type=jnp.float32
    )
    grad_probs = jnp.einsum(
        "qhd,khd->hqk", grad_mixed, value_rows, preferred_element_type=jnp.float32
    )
    inner_sum = jnp.sum(probs * grad_probs, axis=-1, keepdims=True)
    grad_raw = (probs * (grad_probs - inner_sum) * scale).astype(jnp.bfloat16)
    query_rows_gradient = jnp.einsum(
        "hqk,khd->qhd", grad_raw, key_rows, preferred_element_type=jnp.float32
    )
    grad_keys = jnp.einsum("hqk,qhd->khd", grad_raw, query_rows, preferred_element_type=jnp.float32)
    return (
        query_rows_gradient.astype(jnp.bfloat16),
        grad_keys.astype(jnp.bfloat16),
        value_rows_gradient.astype(jnp.bfloat16),
    )


def local(
    inputs,
    segment_ids,
    cotangent,
    qkv_weight,
    out_weight,
    up_weight,
    down_weight,
    query_bias_vector,
    value_bias_vector,
    out_bias,
    gain_one,
    shift_one,
    up_bias,
    down_bias,
    gain_two,
    shift_two,
    query_down,
    query_up_weight,
    value_down,
    value_up_weight,
):
    vector_shards = jnp.stack(
        [
            query_bias_vector,
            value_bias_vector,
            out_bias,
            gain_one,
            shift_one,
            down_bias,
            gain_two,
            shift_two,
        ]
    )
    qkv_full, out_full, up_full, down_full, vector_full, up_bias_full = fetch_forward(
        qkv_weight, out_weight, up_weight, down_weight, vector_shards, up_bias
    )
    vectors = vector_full.astype(jnp.float32)
    packs, seq_len, width = inputs.shape
    rows = packs * seq_len
    flat_in = inputs.reshape(rows, width)
    flat_float = flat_in.astype(jnp.float32)
    projected_rows = jnp.dot(flat_in, qkv_full, preferred_element_type=jnp.float32)
    query_rank_rows = jnp.dot(flat_in, query_down, preferred_element_type=jnp.float32)
    value_rank_rows = jnp.dot(flat_in, value_down, preferred_element_type=jnp.float32)
    query_up_weight_float = query_up_weight.astype(jnp.float32)
    value_up_weight_float = value_up_weight.astype(jnp.float32)
    query_rows = (
        projected_rows[:, :width]
        + vectors[0]
        + adapter_scale
        * jnp.dot(query_rank_rows, query_up_weight_float, precision=highest_precision_mode)
    ).astype(jnp.bfloat16)
    key_rows = projected_rows[:, width : 2 * width].astype(jnp.bfloat16)
    value_rows = (
        projected_rows[:, 2 * width :]
        + vectors[1]
        + adapter_scale
        * jnp.dot(value_rank_rows, value_up_weight_float, precision=highest_precision_mode)
    ).astype(jnp.bfloat16)
    head_shape = (packs, seq_len, HEADS, HEAD_DIM)
    queries_heads = query_rows.reshape(head_shape)
    keys_heads = key_rows.reshape(head_shape)
    values_heads = value_rows.reshape(head_shape)
    attended, log_total = lax.map(
        attend_pack, (queries_heads, keys_heads, values_heads, segment_ids)
    )
    attended_low = attended.reshape(rows, width).astype(jnp.bfloat16)
    hidden_one = (
        flat_float
        + jnp.dot(attended_low, out_full, preferred_element_type=jnp.float32)
        + vectors[2]
    )
    normed_one = layer_norm(hidden_one, vectors[3], vectors[4])
    upper = jnp.dot(
        normed_one.astype(jnp.bfloat16), up_full, preferred_element_type=jnp.float32
    ) + up_bias_full.astype(jnp.float32)
    activated, gelu_pull = jax.vjp(gelu_exact, upper)
    hidden_two = (
        normed_one
        + jnp.dot(activated.astype(jnp.bfloat16), down_full, preferred_element_type=jnp.float32)
        + vectors[5]
    )
    output = layer_norm(hidden_two, vectors[6], vectors[7]).astype(jnp.bfloat16)
    gain_shards = jnp.stack([gain_one, gain_two])
    qkv_back, out_back, up_back, down_back, gain_back = fetch_backward(
        qkv_weight, out_weight, up_weight, down_weight, gain_shards
    )
    gain_back = gain_back.astype(jnp.float32)
    gain_back_one, gain_back_two = (gain_back[0], gain_back[1])
    grad_out = cotangent.reshape(rows, width).astype(jnp.float32)
    normed_again, pull_two = jax.vjp(partial(layer_norm, gain=gain_back_two, shift=0.0), hidden_two)
    (grad_two,) = pull_two(grad_out)
    grad_act = jnp.dot(
        grad_two.astype(jnp.bfloat16), down_back.T, preferred_element_type=jnp.float32
    )
    (grad_upper,) = gelu_pull(grad_act)
    grad_normed = grad_two + jnp.dot(
        grad_upper.astype(jnp.bfloat16), up_back.T, preferred_element_type=jnp.float32
    )
    first_again, pull_one = jax.vjp(partial(layer_norm, gain=gain_back_one, shift=0.0), hidden_one)
    (grad_one,) = pull_one(grad_normed)
    grad_mixed = jnp.dot(
        grad_one.astype(jnp.bfloat16), out_back.T, preferred_element_type=jnp.float32
    ).astype(jnp.bfloat16)
    query_rows_gradient, grad_keys, value_rows_gradient = lax.map(
        attend_back,
        (
            queries_heads,
            keys_heads,
            values_heads,
            segment_ids,
            log_total,
            grad_mixed.reshape(head_shape),
        ),
    )
    query_rows_gradient = query_rows_gradient.reshape(rows, width)
    value_rows_gradient = value_rows_gradient.reshape(rows, width)
    grad_project = jnp.concatenate(
        [query_rows_gradient, grad_keys.reshape(rows, width), value_rows_gradient], axis=1
    )
    query_rank_gradient = adapter_scale * jnp.dot(
        query_rows_gradient, query_up_weight.T, preferred_element_type=jnp.float32
    )
    value_rank_gradient = adapter_scale * jnp.dot(
        value_rows_gradient, value_up_weight.T, preferred_element_type=jnp.float32
    )
    grad_rows = grad_one + jnp.dot(grad_project, qkv_back.T, preferred_element_type=jnp.float32)
    grad_rows = grad_rows + jnp.dot(
        query_rank_gradient, query_down.astype(jnp.float32).T, precision=highest_precision_mode
    )
    grad_rows = grad_rows + jnp.dot(
        value_rank_gradient, value_down.astype(jnp.float32).T, precision=highest_precision_mode
    )
    term_query_up = jnp.dot(
        query_rank_rows.T,
        adapter_scale * query_rows_gradient.astype(jnp.float32),
        precision=highest_precision_mode,
    )
    term_value_up = jnp.dot(
        value_rank_rows.T,
        adapter_scale * value_rows_gradient.astype(jnp.float32),
        precision=highest_precision_mode,
    )
    term_query_down = jnp.dot(flat_float.T, query_rank_gradient, precision=highest_precision_mode)
    term_value_down = jnp.dot(flat_float.T, value_rank_gradient, precision=highest_precision_mode)
    sum_query_down, sum_query_up, sum_value_down, sum_value_up = lax.psum(
        (term_query_down, term_query_up, term_value_down, term_value_up), ("dp", "fsdp")
    )
    return (
        output.reshape(packs, seq_len, width),
        grad_rows.reshape(packs, seq_len, width),
        sum_query_down,
        sum_query_up,
        sum_value_down,
        sum_value_up,
    )


def solution(mesh):
    in_specs = (
        P(("dp", "fsdp"), None, None),
        P(("dp", "fsdp"), None),
        P(("dp", "fsdp"), None, None),
        P(("dp", "fsdp"), None),
        P(("dp", "fsdp"), None),
        P(("dp", "fsdp"), None),
        P(("dp", "fsdp"), None),
        P(("dp", "fsdp")),
        P(("dp", "fsdp")),
        P(("dp", "fsdp")),
        P(("dp", "fsdp")),
        P(("dp", "fsdp")),
        P(("dp", "fsdp")),
        P(("dp", "fsdp")),
        P(("dp", "fsdp")),
        P(("dp", "fsdp")),
        P(),
        P(),
        P(),
        P(),
    )
    out_specs = (P(("dp", "fsdp"), None, None), P(("dp", "fsdp"), None, None), P(), P(), P(), P())
    return jax.shard_map(local, mesh=mesh, in_specs=in_specs, out_specs=out_specs, check_vma=False)
```

profile of v0, /device:TPU:8, one launch (start us, length us, event | category | flops | bytes accessed | tf_op | source)
XLA Modules:
  0.0 645.6 jit_solution(10639014909072017310)
XLA Ops:
  11.6 57.1 %all-gather = bf16[32,24,8]{1,2,0:T(8,128)(2,1)S(1)} all-gather(bf16[1,24,8]{1,2,0:T(8,128)(2,1)S(1)} %bitcast.216), channel_id=1, replica_groups=mesh['dp'=8,'fsdp'=4] {'dp','fsdp'}, dimensions={0}, use_global_device_ids=true | all-gather | bytes 12672 | tf_op jit(solution)/shard_map/all_gather | solution.py:30
  69.7 1.9 fusion.158
  71.6 1.9 fusion.159
  73.8 50.2 %all-reduce = bf16[3072]{0:T(1024)(128)(2,1)S(1)} all-reduce(bf16[3072]{0:T(1024)(128)(2,1)S(1)} %dynamic-update-slice), channel_id=1, replica_groups=mesh['dp'=8,'fsdp'=4] {'dp','fsdp'}, use_global_device_ids=true, to_apply=%add | all-reduce | flops 3072 | bytes 12288
  124.7 51.4 %all-gather.1 = bf16[32,24,2]{1,2,0:T(2,128)(2,1)S(1)} all-gather(bf16[1,24,2]{1,2,0:T(2,128)(2,1)S(1)} %maximum_bitcast_fusion), channel_id=1, replica_groups=mesh['dp'=8,'fsdp'=4] {'dp','fsdp'}, dimensions={0}, use_global_device_ids=true | all-gather | bytes 3168 | tf_op jit(solution)/shard_map/all_gather | solution.py:41
  177.0 5.8 fusion.157
  183.0 3.4 copy-done.11
  186.5 2.7 fusion.122
  189.1 2.2 copy.92
  191.3 2.4 reshape.185
  193.7 2.9 copy.95
  196.6 4.6 fusion.120
  201.2 1.7 copy.93
  202.9 2.4 reshape.186
  205.2 1.7 copy.96
  207.0 1.6 copy.94
  208.6 3.8 reshape.187
  212.4 1.7 copy.97
  214.2 23.0 %while.26 = (s32[]{:T(128)}, bf16[2,512,12,64]{1,3,2,0:T(8,128)(2,1)}, f32[2,12,512]{2,1,0:T(8,128)}, bf16[2,512,12,64]{1,3,2,0:T(8,128)(2,1)}, s32[2,512]{1,0:T...) while((s32[]{:T(128)}, ...), condition=%wide.region_3.4_spmd, body=%wide.region_0.3_spmd.sunk | while | flops 849602560 | bytes 49250932 | solution.py:156
  215.1 2.1 fusion.216
  217.2 3.1 fusion.217
  221.0 4.6 bitcast_dynamic-update-slice_fusion.4
  226.5 2.1 fusion.216
  228.6 3.1 fusion.217
  232.4 4.6 bitcast_dynamic-update-slice_fusion.4
  237.2 3.0 copy.98
  240.2 1.6 copy.115
  241.8 3.9 fusion.155
  245.7 1.6 copy-done.7
  248.0 36.6 %fusion.103 = (f32[1024,3072]{1,0:T(8,128)}, f32[1024,3072]{1,0:T(8,128)}) fusion(f32[3072]{0:T(1024)S(1)} %copy-done.29, bf16[768,3072]{1,0:T(8,128)(2,1)} %all-gather.11.cloned.1.call-done, f32[1024,768]{1,0:T(8,128)} %copy-done.7, f32[768]{0:T(1024)S(1)} %copy-done.31, f32[768]{0:T(1024)S(1)} %copy-done.32, f32[1024]{0:T(1024)S(1)} %fusion.144, ...), kind=kOutput, calls=%fused_computation.80 | convolution fusion | flops 5033951232 | bytes 33056768 | tf_op jit(solution)/shard_map/dot_general | solution.py:166
  284.6 16.2 %fusion.156 = (f32[1024]{0:T(1024)S(1)}, f32[1024,768]{1,0:T(8,128)S(1)}) fusion(f32[768]{0:T(1024)S(1)} %copy-done.30, bf16[3072,768]{1,0:T(8,128)(2,1)} %all-gather.13.cloned.1.call-done, f32[1024,3072]{1,0:T(8,128)} %get-tuple-element.232, f32[1024,3072]{1,0:T(8,128)} %get-tuple-element.233, f32[3072]{0:T(1024)S(1)} %copy-done.29, ...), kind=kOutput, calls=%fused_computation.183 | convolution fusion | flops 4849925120 | bytes 36209664 | tf_op jit(solution)/shard_map/dot_general | solution.py:172
  301.9 3.2 fusion.154
  305.2 23.1 %multiply_reduce_fusion.1 = (f32[1024]{0:T(1024)S(1)}, f32[1024,768]{1,0:T(8,128)}) fusion(f32[1024,768]{1,0:T(8,128)} %copy-done.7, f32[1024]{0:T(1024)S(1)} %broadcast_multiply_fusion.1, f32[768]{0:T(1024)S(1)} %copy-done.34, bf16[768,3072]{1,0:T(8,128)(2,1)} %all-gather.11.cloned.1.call-done, f32[1024,3072]{1,0:T(8,128)} %get-tuple-element.232, ...), kind=kOutput, calls=%fused_computation.126 | convolution fusion | flops 9717152768 | bytes 44067840 | tf_op jit(solution)/shard_map/dot_general | solution.py:189
  328.3 3.6 fusion.153
  331.9 1.7 copy-done.9
  333.7 2.6 convolution_convert_fusion
  336.3 2.6 copy.101
  338.9 3.8 reshape.189
  342.7 2.9 copy.104
  345.6 126.3 %while.27 = (s32[]{:T(128)}, bf16[2,512,12,64]{1,3,2,0:T(8,128)(2,1)}, bf16[2,512,12,64]{1,3,2,0:T(8,128)(2,1)}, bf16[2,512,12,64]{1,3,2,0:T(8,128)(2,1)}, bf16[...) while((s32[]{:T(128)}, ...), condition=%wide.region_14.15_spmd, body=%wide.region_12.14_spmd.sunk | while | flops 2096509952 | bytes 160648368 | solution.py:197
  345.8 6.4 fusion.229
  352.2 6.3 fusion.228
  360.2 20.3 %fusion.231 = bf16[2,512,12,64]{1,3,2,0:T(8,128)(2,1)} fusion(bf16[2,512,12,64]{1,3,2,0:T(8,128)(2,1)} %get-tuple-element.383, s32[]{:T(128)} %get-tuple-element.381, f32[12,512,512]{1,2,0:T(8,128)} %fusion.228, f32[12,512,512]{1,2,0:T(8,128)} %fusion.229, f32[12,512]{1,0:T(8,128)S(1)} %dynamic-slice_bitcast_fusion.2, ...), kind=kOutput, calls=%fused_computation.44.clone.1 | convolution fusion | flops 437656064 | bytes 52495360 | tf_op jit(solution)/shard_map/while/body/eval_jaxpr/hqk,qhd->khd/dot_general | solution.py:84
  380.5 20.1 %fusion.230 = bf16[2,512,12,64]{1,3,2,0:T(8,128)(2,1)} fusion(bf16[2,512,12,64]{1,3,2,0:T(8,128)(2,1)} %get-tuple-element.382, s32[]{:T(128)} %get-tuple-element.381, f32[12,512,512]{1,2,0:T(8,128)} %fusion.228, f32[12,512,512]{1,2,0:T(8,128)} %fusion.229, f32[12,512]{1,0:T(8,128)S(1)} %dynamic-slice_bitcast_fusion.2, ...), kind=kOutput, calls=%fused_computation.46.clone.1 | convolution fusion | flops 437656064 | bytes 52495360 | tf_op jit(solution)/shard_map/while/body/eval_jaxpr/hqk,khd->qhd/dot_general | solution.py:81
  400.6 8.3 %fusion.232 = bf16[2,512,12,64]{1,3,2,0:T(8,128)(2,1)} fusion(bf16[2,512,12,64]{1,3,2,0:T(8,128)(2,1)} %get-tuple-element.384, s32[]{:T(128)} %get-tuple-element.381, f32[12,512,512]{1,2,0:T(8,128)} %fusion.229, f32[12,512]{1,0:T(8,128)S(1)} %dynamic-slice_bitcast_fusion.2, pred[512,512]{0,1:T(8,128)(4,1)S(1)} %broadcast_compare_fusion.5, ...), kind=kOutput, calls=%fused_computation.48.clone.1 | convolution fusion | flops 415629312 | bytes 14443520 | tf_op jit(solution)/shard_map/while/body/eval_jaxpr/hqk,qhd->khd/dot_general | solution.py:73
  408.9 6.4 fusion.229
  415.3 6.3 fusion.228
  423.3 20.3 %fusion.231 = bf16[2,512,12,64]{1,3,2,0:T(8,128)(2,1)} fusion(bf16[2,512,12,64]{1,3,2,0:T(8,128)(2,1)} %get-tuple-element.383, s32[]{:T(128)} %get-tuple-element.381, f32[12,512,512]{1,2,0:T(8,128)} %fusion.228, f32[12,512,512]{1,2,0:T(8,128)} %fusion.229, f32[12,512]{1,0:T(8,128)S(1)} %dynamic-slice_bitcast_fusion.2, ...), kind=kOutput, calls=%fused_computation.44.clone.1 | convolution fusion | flops 437656064 | bytes 52495360 | tf_op jit(solution)/shard_map/while/body/eval_jaxpr/hqk,qhd->khd/dot_general | solution.py:84
  443.6 20.1 %fusion.230 = bf16[2,512,12,64]{1,3,2,0:T(8,128)(2,1)} fusion(bf16[2,512,12,64]{1,3,2,0:T(8,128)(2,1)} %get-tuple-element.382, s32[]{:T(128)} %get-tuple-element.381, f32[12,512,512]{1,2,0:T(8,128)} %fusion.228, f32[12,512,512]{1,2,0:T(8,128)} %fusion.229, f32[12,512]{1,0:T(8,128)S(1)} %dynamic-slice_bitcast_fusion.2, ...), kind=kOutput, calls=%fused_computation.46.clone.1 | convolution fusion | flops 437656064 | bytes 52495360 | tf_op jit(solution)/shard_map/while/body/eval_jaxpr/hqk,khd->qhd/dot_general | solution.py:81
  463.7 8.3 %fusion.232 = bf16[2,512,12,64]{1,3,2,0:T(8,128)(2,1)} fusion(bf16[2,512,12,64]{1,3,2,0:T(8,128)(2,1)} %get-tuple-element.384, s32[]{:T(128)} %get-tuple-element.381, f32[12,512,512]{1,2,0:T(8,128)} %fusion.229, f32[12,512]{1,0:T(8,128)S(1)} %dynamic-slice_bitcast_fusion.2, pred[512,512]{0,1:T(8,128)(4,1)S(1)} %broadcast_compare_fusion.5, ...), kind=kOutput, calls=%fused_computation.48.clone.1 | convolution fusion | flops 415629312 | bytes 14443520 | tf_op jit(solution)/shard_map/while/body/eval_jaxpr/hqk,qhd->khd/dot_general | solution.py:73
  472.0 3.0 copy.108
  475.4 1.6 copy.110
  477.3 1.6 copy.106
  479.0 1.6 copy.116
  480.6 2.9 copy.109
  483.5 1.8 convolution_multiply_fusion.1
  486.7 3.1 fusion.160
  489.8 2.4 fusion.126
  492.2 2.4 fusion.129
  495.9 3.1 copy.107
  499.0 1.6 copy.117
  500.7 6.6 %fusion.113 = f32[1024,768]{1,0:T(8,128)S(1)} fusion(bf16[768,2304]{1,0:T(8,128)(2,1)} %all-gather.7.cloned.1.call-done, bf16[1024,768]{0,1:T(8,128)(2,1)S(1)} %bitcast.200, bf16[1024,768]{0,1:T(8,128)(2,1)} %bitcast.210, bf16[1024,768]{0,1:T(8,128)(2,1)S(1)} %bitcast.203), kind=kOutput, calls=%fused_computation.102 | convolution fusion | flops 3638034432 | bytes 11403264 | tf_op jit(solution)/shard_map/dot_general | solution.py:219
  507.3 3.5 add_add_fusion.2
  510.8 122.5 %all-reduce.4.cloned.1.call-done = (f32[768,8]{0,1:T(8,128)}, f32[8,768]{1,0:T(8,128)}, f32[768,8]{0,1:T(8,128)}, f32[8,768]{1,0:T(8,128)}) async-done(((f32[768,8]{0,1:T(8,128)}, f32[8,768]{1,0:T(8,128)}, f32[768,8]{0,1:T(8,128)}, f32[8,768]{1,0:T(8,128)}), (f32[768,8]{0,1:T(8,128)}, f32[8,768]{1,0:T(8,128)}, f32[768,8]{0,1:T(8,128)}, f32[8,768]{1,0:T(8,128)})) %all-reduce.4.cloned.1.call-update) | async-done | bytes 98320 | tf_op jit(solution)/shard_map/psum | solution.py:238
  (139 shorter events, 24.2 us)
Async XLA Ops:
  7.2 179.3 %copy-start = (bf16[8,768]{1,0:T(8,128)(2,1)S(1)}, bf16[8,768]{1,0:T(8,128)(2,1)}, u32[]{:S(2)}) copy-start(bf16[8,768]{1,0:T(8,128)(2,1)} %param.43) | copy-start | bytes 36868
  7.2 169.8 %copy-start.1 = (bf16[2,512,768]{2,1,0:T(8,128)(2,1)S(1)}, bf16[2,512,768]{2,1,0:T(8,128)(2,1)}, u32[]{:S(2)}) copy-start(bf16[2,512,768]{2,1,0:T(8,128)(2,1)} %param.24) | copy-start | bytes 4718596
  7.2 66.4 %copy-start.36 = (bf16[96]{0:T(256)(128)(2,1)S(1)}, bf16[96]{0:T(256)(128)(2,1)}, u32[]{:S(2)}) copy-start(bf16[96]{0:T(256)(128)(2,1)} %param.36) | copy-start | bytes 580
  7.2 169.8 %all-gather.7.cloned.1.call-start = ((), (), s32[]{:S(2)}) async-start(), calls=%async_computation | async-start | bytes 3649536 | tf_op jit(solution)/shard_map/all_gather | solution.py:26
  7.9 233.8 %all-gather.9.cloned.1.call-start = ((), (), s32[]{:S(2)}) async-start(), calls=%async_computation.1 | async-start | bytes 1216512 | tf_op jit(solution)/shard_map/all_gather | solution.py:27
  8.7 239.2 %all-gather.11.cloned.1.call-start = ((), (), s32[]{:S(2)}) async-start(), calls=%async_computation.2 | async-start | bytes 4866048 | tf_op jit(solution)/shard_map/all_gather | solution.py:28
  9.4 275.1 %all-gather.13.cloned.1.call-start = ((), (), s32[]{:S(2)}) async-start(), calls=%async_computation.3 | async-start | bytes 4866048 | tf_op jit(solution)/shard_map/all_gather | solution.py:29
  10.0 623.3 %all-reduce.4.cloned.1.call-start = ((), (), s32[]{:S(2)}) async-start(), calls=%async_computation.4 | async-start | bytes 196608 | tf_op jit(solution)/shard_map/psum | solution.py:238
  71.6 111.4 %copy-start.18 = (f32[1024,8]{0,1:T(8,128)}, f32[1024,8]{0,1:T(8,128)S(1)}, u32[]{:S(2)}) copy-start(f32[1024,8]{0,1:T(8,128)S(1)} %fusion.158) | copy-start | bytes 98308
  73.5 123.0 %copy-start.16 = (f32[1024,8]{0,1:T(8,128)}, f32[1024,8]{0,1:T(8,128)S(1)}, u32[]{:S(2)}) copy-start(f32[1024,8]{0,1:T(8,128)S(1)} %fusion.159) | copy-start | bytes 98308
  182.8 3.6 copy-start.11
  191.3 5.3 copy-start.20
  217.2 3.8 copy-start.3
  228.6 3.8 copy-start.3
  237.1 4.6 copy-start.33
  245.7 1.7 copy-start.7
  245.7 2.2 copy-start.29
  245.7 2.2 copy-start.31
  245.7 2.2 copy-start.32
  247.9 36.6 %copy-start.30 = (f32[768]{0:T(1024)S(1)}, f32[768]{0:T(1024)}, u32[]{:S(2)}) copy-start(f32[768]{0:T(1024)} %get-tuple-element.175) | copy-start | bytes 9220
  284.6 16.3 %copy-start.12 = (bf16[2,512,768]{2,1,0:T(8,128)(2,1)S(1)}, bf16[2,512,768]{2,1,0:T(8,128)(2,1)}, u32[]{:S(2)}) copy-start(bf16[2,512,768]{2,1,0:T(8,128)(2,1)} %param.26) | copy-start | bytes 4718596
  284.6 16.3 %copy-start.24 = (f32[768]{0:T(1024)S(1)}, f32[768]{0:T(1024)}, u32[]{:S(2)}) copy-start(f32[768]{0:T(1024)} %get-tuple-element.182) | copy-start | bytes 9220
  300.8 1.1 copy-start.25
  300.8 1.1 copy-start.26
  301.9 3.3 copy-start.34
  328.3 5.3 copy-start.35
  331.9 1.8 copy-start.9
  331.9 1.7 copy-start.27
  345.8 6.4 copy-start.4
  345.8 6.4 copy-start.5
  408.9 6.4 copy-start.4
  408.9 6.4 copy-start.5
  475.4 1.9 copy-start.15
  478.9 4.5 copy-start.21
  480.6 4.8 copy-start.2
  480.6 6.1 copy-start.22
  483.5 6.3 copy-start.13
  483.5 6.3 copy-start.19
  485.4 6.8 %copy-start.14 = (bf16[1024,768]{1,0:T(8,128)(2,1)S(1)}, bf16[1024,768]{1,0:T(8,128)(2,1)}, u32[]{:S(2)}) copy-start(bf16[1024,768]{1,0:T(8,128)(2,1)} %copy.109) | copy-start | bytes 4718596
  485.4 6.8 %copy-start.17 = (f32[1024,8]{0,1:T(8,128)S(1)}, f32[1024,8]{0,1:T(8,128)}, u32[]{:S(2)}) copy-start(f32[1024,8]{0,1:T(8,128)} %copy-done.16) | copy-start | bytes 98308
  495.9 4.8 copy-start.6
  500.7 6.6 %copy-start.8 = (f32[1024,768]{1,0:T(8,128)S(1)}, f32[1024,768]{1,0:T(8,128)}, u32[]{:S(2)}) copy-start(f32[1024,768]{1,0:T(8,128)} %fusion.160) | copy-start | bytes 9437188
  500.7 6.6 %copy-start.10 = (f32[1024,768]{1,0:T(8,128)S(1)}, f32[1024,768]{1,0:T(8,128)}, u32[]{:S(2)}) copy-start(f32[1024,768]{1,0:T(8,128)} %copy-done.9) | copy-start | bytes 9437188
  500.7 6.6 %copy-start.23 = (bf16[768,8]{0,1:T(8,128)(2,1)S(1)}, bf16[768,8]{0,1:T(8,128)(2,1)}, u32[]{:S(2)}) copy-start(bf16[768,8]{0,1:T(8,128)(2,1)} %param.42) | copy-start | bytes 36868
  500.7 6.6 %copy-start.28 = (f32[1024]{0:T(1024)S(1)}, f32[1024]{0:T(1024)}, u32[]{:S(2)}) copy-start(f32[1024]{0:T(1024)} %copy-done.27) | copy-start | bytes 12292
Sparse Core Ops, SparseCore 0:
  10.9 61.1 all-gather.6
  75.0 52.4 all-gather.8
  130.4 64.2 all-gather.10
  197.4 62.3 all-gather.12
  500.8 132.4 all-reduce.3
where the time goes:
time: 652 us; the launch traced here: 646 us
  matrix products  258 us (40%)
  blocking collectives  159 us (24%)
  waiting for transfers between devices  125 us (19%)
  local copies, waits for them, and re-layouts  70 us (11%)
  other arithmetic  18.1 us (3%)
  between operations  14.7 us (2%)
    psum x1, waiting for transfers between devices, local(): lax.psum((term_query_down, term_query_up, term_value_down, term_value_up)...  123 us
    all_gather x1, blocking collectives, fetch_forward(): lax.all_gather(vectors, ('dp', 'fsdp'), axis=1, tiled=True)  57.1 us
    all_gather x1, blocking collectives, fetch_backward(): lax.all_gather(gains, ('dp', 'fsdp'), axis=1, tiled=True)  51.4 us
    unnamed x1, blocking collectives  50.2 us
    dot_general x2, matrix products, attend_back(): jnp.einsum('hqk,qhd->khd', grad_raw, query_rows, preferred_element_type=j...  40.7 us
    dot_general x2, matrix products, attend_back(): jnp.einsum('hqk,khd->qhd', grad_raw, key_rows, preferred_element_type=jnp...  40.1 us
    dot_general x1, matrix products, local(): jnp.dot(normed_one.astype(jnp.bfloat16), up_full, preferred_element_type=...  36.6 us
    dot_general x1, matrix products, local(): jnp.dot(grad_upper.astype(jnp.bfloat16), up_back.T, preferred_element_typ...  23.1 us
  transfers between devices with their start and end apart: 5, of which 1 were waited for; matrix products, arithmetic and copies ran while one was open for 19% of the time, Pallas kernels for 0%

commit v1 on v0

--- a/solution.py
+++ b/solution.py
@@ -9,6 +9,11 @@
 highest_precision_mode = lax.Precision.HIGHEST
 norm_epsilon = 1e-05
 adapter_scale = 2.0
+
+
+def supply_all_leaves_in(mesh_name, block_in, shard_axis):
+    state_now = jax.lax.psum(jax.lax.psum(block_in, mesh_name), shard_axis)
+    return state_now
 
 
 def layer_norm(value_rows, gain, shift):
@@ -235,8 +240,10 @@
     )
     term_query_down = jnp.dot(flat_float.T, query_rank_gradient, precision=highest_precision_mode)
     term_value_down = jnp.dot(flat_float.T, value_rank_gradient, precision=highest_precision_mode)
-    sum_query_down, sum_query_up, sum_value_down, sum_value_up = lax.psum(
-        (term_query_down, term_query_up, term_value_down, term_value_up), ("dp", "fsdp")
+    sum_query_down, sum_query_up, sum_value_down, sum_value_up = supply_all_leaves_in(
+        "fsdp",
+        block_in=(term_query_down, term_query_up, term_value_down, term_value_up),
+        shard_axis="dp",
     )
     return (
         output.reshape(packs, seq_len, width),

time: 652 us -> 622 us (0.954)
  waiting for transfers between devices: 125 us -> 93.8 us
    psum x1 -> x2, waiting for transfers between devices: 123 us -> 91.2 us  [supply_all_leaves_in(): state_now = jax.lax.psum(jax.lax.psum(block_in, mesh_name), shard_axis)]
    unnamed x78 -> x70, local copies, waits for them, and re-layouts: 17.8 us -> 16.6 us
  transfers between devices with their start and end apart: 5 -> 6, of which waited for: 1 -> 2; matrix products, arithmetic and copies ran while one was open for 19% -> 20% of each run, Pallas kernels for 0% -> 0%
where the time goes in v1:
time: 622 us; the launch traced here: 615 us
  matrix products  261 us (42%)
  blocking collectives  159 us (26%)
  waiting for transfers between devices  93.8 us (15%)
  local copies, waits for them, and re-layouts  67.2 us (11%)
  other arithmetic  18.1 us (3%)
  between operations  14.8 us (2%)
    psum x2, waiting for transfers between devices, supply_all_leaves_in(): state_now = jax.lax.psum(jax.lax.psum(block_in, mesh_name), shard_axis)  91.2 us
    all_gather x1, blocking collectives, fetch_forward(): lax.all_gather(vectors, ('dp', 'fsdp'), axis=1, tiled=True)  57.1 us
    all_gather x1, blocking collectives, fetch_backward(): lax.all_gather(gains, ('dp', 'fsdp'), axis=1, tiled=True)  51.5 us
    unnamed x1, blocking collectives  50.2 us
    dot_general x2, matrix products, attend_back(): jnp.einsum('hqk,qhd->khd', grad_raw, query_rows, preferred_element_type=j...  40.7 us
    dot_general x2, matrix products, attend_back(): jnp.einsum('hqk,khd->qhd', grad_raw, key_rows, preferred_element_type=jnp...  40.1 us
    dot_general x1, matrix products, local(): jnp.dot(normed_one.astype(jnp.bfloat16), up_full, preferred_element_type=...  36.6 us
    dot_general x1, matrix products, local(): jnp.dot(grad_upper.astype(jnp.bfloat16), up_back.T, preferred_element_typ...  23.1 us
  transfers between devices with their start and end apart: 6, of which 2 were waited for; matrix products, arithmetic and copies ran while one was open for 20% of the time, Pallas kernels for 0%

profile of v1, /device:TPU:8, one launch (start us, length us, event | category | flops | bytes accessed | tf_op | source)
XLA Modules:
  0.0 615.3 jit_solution(17712288179426306586)
XLA Ops:
  11.6 57.1 %all-gather = bf16[32,24,8]{1,2,0:T(8,128)(2,1)S(1)} all-gather(bf16[1,24,8]{1,2,0:T(8,128)(2,1)S(1)} %bitcast.216), channel_id=1, replica_groups=mesh['dp'=8,'fsdp'=4] {'dp','fsdp'}, dimensions={0}, use_global_device_ids=true | all-gather | bytes 12672 | tf_op jit(solution)/shard_map/all_gather | solution.py:35
  69.7 1.9 fusion.158
  71.6 1.9 fusion.159
  73.8 50.2 %all-reduce = bf16[3072]{0:T(1024)(128)(2,1)S(1)} all-reduce(bf16[3072]{0:T(1024)(128)(2,1)S(1)} %dynamic-update-slice), channel_id=1, replica_groups=mesh['dp'=8,'fsdp'=4] {'dp','fsdp'}, use_global_device_ids=true, to_apply=%add | all-reduce | flops 3072 | bytes 12288
  124.6 51.5 %all-gather.1 = bf16[32,24,2]{1,2,0:T(2,128)(2,1)S(1)} all-gather(bf16[1,24,2]{1,2,0:T(2,128)(2,1)S(1)} %maximum_bitcast_fusion), channel_id=1, replica_groups=mesh['dp'=8,'fsdp'=4] {'dp','fsdp'}, dimensions={0}, use_global_device_ids=true | all-gather | bytes 3168 | tf_op jit(solution)/shard_map/all_gather | solution.py:46
  177.0 5.8 fusion.157
  183.0 3.4 copy-done.8
  186.5 2.7 fusion.122
  189.2 2.0 copy.92
  191.2 2.4 reshape.185
  193.5 2.9 copy.95
  196.4 4.6 fusion.120
  201.0 1.7 copy.93
  202.7 2.4 reshape.186
  205.1 1.7 copy.96
  206.8 1.6 copy.94
  208.5 3.8 reshape.187
  212.3 1.7 copy.97
  214.0 23.3 %while.26 = (s32[]{:T(128)}, bf16[2,512,12,64]{1,3,2,0:T(8,128)(2,1)}, f32[2,12,512]{2,1,0:T(8,128)}, bf16[2,512,12,64]{1,3,2,0:T(8,128)(2,1)}, s32[2,512]{1,0:T...) while((s32[]{:T(128)}, ...), condition=%wide.region_3.4_spmd, body=%wide.region_0.3_spmd.sunk | while | flops 849602560 | bytes 49250932 | solution.py:161
  215.0 2.1 fusion.216
  217.1 3.1 fusion.217
  220.8 4.6 bitcast_dynamic-update-slice_fusion.4
  226.4 2.1 fusion.216
  228.5 3.1 fusion.217
  232.2 4.6 bitcast_dynamic-update-slice_fusion.4
  237.4 3.0 copy.98
  240.4 1.6 copy.115
  242.0 3.9 fusion.155
  246.0 1.6 copy-done.6
  248.2 36.6 %fusion.103 = (f32[1024,3072]{1,0:T(8,128)}, f32[1024,3072]{1,0:T(8,128)}) fusion(f32[3072]{0:T(1024)S(1)} %copy-done.25, bf16[768,3072]{1,0:T(8,128)(2,1)} %all-gather.11.cloned.1.call-done, f32[1024,768]{1,0:T(8,128)} %copy-done.6, f32[768]{0:T(1024)S(1)} %copy-done.27, f32[768]{0:T(1024)S(1)} %copy-done.28, f32[1024]{0:T(1024)S(1)} %fusion.144, ...), kind=kOutput, calls=%fused_computation.80 | convolution fusion | flops 5033951232 | bytes 33056768 | tf_op jit(solution)/shard_map/dot_general | solution.py:171
  284.8 16.0 %fusion.156 = (f32[1024]{0:T(1024)S(1)}, f32[1024,768]{1,0:T(8,128)S(1)}) fusion(f32[768]{0:T(1024)S(1)} %copy-done.26, bf16[3072,768]{1,0:T(8,128)(2,1)} %all-gather.13.cloned.1.call-done, f32[1024,3072]{1,0:T(8,128)} %get-tuple-element.236, f32[1024,3072]{1,0:T(8,128)} %get-tuple-element.237, f32[3072]{0:T(1024)S(1)} %copy-done.25, ...), kind=kOutput, calls=%fused_computation.183 | convolution fusion | flops 4849925120 | bytes 36209664 | tf_op jit(solution)/shard_map/dot_general | solution.py:177
  302.0 3.2 fusion.154
  305.2 23.1 %multiply_reduce_fusion.1 = (f32[1024]{0:T(1024)S(1)}, f32[1024,768]{1,0:T(8,128)}) fusion(f32[1024,768]{1,0:T(8,128)} %copy-done.6, f32[1024]{0:T(1024)S(1)} %broadcast_multiply_fusion.1, f32[768]{0:T(1024)S(1)} %copy-done.30, bf16[768,3072]{1,0:T(8,128)(2,1)} %all-gather.11.cloned.1.call-done, f32[1024,3072]{1,0:T(8,128)} %get-tuple-element.236, ...), kind=kOutput, calls=%fused_computation.126 | convolution fusion | flops 9717152768 | bytes 44067840 | tf_op jit(solution)/shard_map/dot_general | solution.py:194
  328.4 3.6 fusion.153
  331.9 1.7 copy-done.7
  333.7 2.6 convolution_convert_fusion
  336.3 2.6 copy.101
  338.9 3.8 reshape.189
  342.7 2.9 copy.104
  345.6 126.8 %while.27 = (s32[]{:T(128)}, bf16[2,512,12,64]{1,3,2,0:T(8,128)(2,1)}, bf16[2,512,12,64]{1,3,2,0:T(8,128)(2,1)}, bf16[2,512,12,64]{1,3,2,0:T(8,128)(2,1)}, bf16[...) while((s32[]{:T(128)}, ...), condition=%wide.region_14.15_spmd, body=%wide.region_12.14_spmd.sunk | while | flops 2096509952 | bytes 160648368 | solution.py:202
  345.9 6.4 %fusion.229 = f32[12,512,512]{1,2,0:T(8,128)} fusion(bf16[2,512,12,64]{1,3,2,0:T(8,128)(2,1)S(1)} %get-tuple-element.402, s32[]{:T(128)} %get-tuple-element.385, bf16[2,512,12,64]{1,3,2,0:T(8,128)(2,1)S(1)} %get-tuple-element.400), kind=kOutput, calls=%fused_computation.54.clone.1 | convolution fusion | flops 402653184 | bytes 14156800 | tf_op jit(solution)/shard_map/while/body/eval_jaxpr/qhd,khd->hqk/dot_general | solution.py:73
  352.3 6.3 %fusion.228 = f32[12,512,512]{1,2,0:T(8,128)} fusion(bf16[2,512,12,64]{1,3,2,0:T(8,128)(2,1)S(1)} %copy-done.4, s32[]{:T(128)} %get-tuple-element.385, bf16[2,512,12,64]{1,3,2,0:T(8,128)(2,1)S(1)} %copy-done.5), kind=kOutput, calls=%fused_computation.49.clone.1 | convolution fusion | flops 402653184 | bytes 14156800 | tf_op jit(solution)/shard_map/while/body/eval_jaxpr/qhd,khd->hqk/dot_general | solution.py:81
  360.3 20.3 %fusion.231 = bf16[2,512,12,64]{1,3,2,0:T(8,128)(2,1)} fusion(bf16[2,512,12,64]{1,3,2,0:T(8,128)(2,1)} %get-tuple-element.387, s32[]{:T(128)} %get-tuple-element.385, f32[12,512,512]{1,2,0:T(8,128)} %fusion.228, f32[12,512,512]{1,2,0:T(8,128)} %fusion.229, f32[12,512]{1,0:T(8,128)S(1)} %dynamic-slice_bitcast_fusion.2, ...), kind=kOutput, calls=%fused_computation.44.clone.1 | convolution fusion | flops 437656064 | bytes 52495360 | tf_op jit(solution)/shard_map/while/body/eval_jaxpr/hqk,qhd->khd/dot_general | solution.py:89
  380.6 20.1 %fusion.230 = bf16[2,512,12,64]{1,3,2,0:T(8,128)(2,1)} fusion(bf16[2,512,12,64]{1,3,2,0:T(8,128)(2,1)} %get-tuple-element.386, s32[]{:T(128)} %get-tuple-element.385, f32[12,512,512]{1,2,0:T(8,128)} %fusion.228, f32[12,512,512]{1,2,0:T(8,128)} %fusion.229, f32[12,512]{1,0:T(8,128)S(1)} %dynamic-slice_bitcast_fusion.2, ...), kind=kOutput, calls=%fused_computation.46.clone.1 | convolution fusion | flops 437656064 | bytes 52495360 | tf_op jit(solution)/shard_map/while/body/eval_jaxpr/hqk,khd->qhd/dot_general | solution.py:86
  400.7 8.3 %fusion.232 = bf16[2,512,12,64]{1,3,2,0:T(8,128)(2,1)} fusion(bf16[2,512,12,64]{1,3,2,0:T(8,128)(2,1)} %get-tuple-element.388, s32[]{:T(128)} %get-tuple-element.385, f32[12,512,512]{1,2,0:T(8,128)} %fusion.229, f32[12,512]{1,0:T(8,128)S(1)} %dynamic-slice_bitcast_fusion.2, pred[512,512]{0,1:T(8,128)(4,1)S(1)} %broadcast_compare_fusion.5, ...), kind=kOutput, calls=%fused_computation.48.clone.1 | convolution fusion | flops 415629312 | bytes 14443520 | tf_op jit(solution)/shard_map/while/body/eval_jaxpr/hqk,qhd->khd/dot_general | solution.py:78
  409.0 6.4 %fusion.229 = f32[12,512,512]{1,2,0:T(8,128)} fusion(bf16[2,512,12,64]{1,3,2,0:T(8,128)(2,1)S(1)} %get-tuple-element.402, s32[]{:T(128)} %get-tuple-element.385, bf16[2,512,12,64]{1,3,2,0:T(8,128)(2,1)S(1)} %get-tuple-element.400), kind=kOutput, calls=%fused_computation.54.clone.1 | convolution fusion | flops 402653184 | bytes 14156800 | tf_op jit(solution)/shard_map/while/body/eval_jaxpr/qhd,khd->hqk/dot_general | solution.py:73
  415.4 6.3 %fusion.228 = f32[12,512,512]{1,2,0:T(8,128)} fusion(bf16[2,512,12,64]{1,3,2,0:T(8,128)(2,1)S(1)} %copy-done.4, s32[]{:T(128)} %get-tuple-element.385, bf16[2,512,12,64]{1,3,2,0:T(8,128)(2,1)S(1)} %copy-done.5), kind=kOutput, calls=%fused_computation.49.clone.1 | convolution fusion | flops 402653184 | bytes 14156800 | tf_op jit(solution)/shard_map/while/body/eval_jaxpr/qhd,khd->hqk/dot_general | solution.py:81
  423.4 20.3 %fusion.231 = bf16[2,512,12,64]{1,3,2,0:T(8,128)(2,1)} fusion(bf16[2,512,12,64]{1,3,2,0:T(8,128)(2,1)} %get-tuple-element.387, s32[]{:T(128)} %get-tuple-element.385, f32[12,512,512]{1,2,0:T(8,128)} %fusion.228, f32[12,512,512]{1,2,0:T(8,128)} %fusion.229, f32[12,512]{1,0:T(8,128)S(1)} %dynamic-slice_bitcast_fusion.2, ...), kind=kOutput, calls=%fused_computation.44.clone.1 | convolution fusion | flops 437656064 | bytes 52495360 | tf_op jit(solution)/shard_map/while/body/eval_jaxpr/hqk,qhd->khd/dot_general | solution.py:89
  443.7 20.1 %fusion.230 = bf16[2,512,12,64]{1,3,2,0:T(8,128)(2,1)} fusion(bf16[2,512,12,64]{1,3,2,0:T(8,128)(2,1)} %get-tuple-element.386, s32[]{:T(128)} %get-tuple-element.385, f32[12,512,512]{1,2,0:T(8,128)} %fusion.228, f32[12,512,512]{1,2,0:T(8,128)} %fusion.229, f32[12,512]{1,0:T(8,128)S(1)} %dynamic-slice_bitcast_fusion.2, ...), kind=kOutput, calls=%fused_computation.46.clone.1 | convolution fusion | flops 437656064 | bytes 52495360 | tf_op jit(solution)/shard_map/while/body/eval_jaxpr/hqk,khd->qhd/dot_general | solution.py:86
  463.7 8.3 %fusion.232 = bf16[2,512,12,64]{1,3,2,0:T(8,128)(2,1)} fusion(bf16[2,512,12,64]{1,3,2,0:T(8,128)(2,1)} %get-tuple-element.388, s32[]{:T(128)} %get-tuple-element.385, f32[12,512,512]{1,2,0:T(8,128)} %fusion.229, f32[12,512]{1,0:T(8,128)S(1)} %dynamic-slice_bitcast_fusion.2, pred[512,512]{0,1:T(8,128)(4,1)S(1)} %broadcast_compare_fusion.5, ...), kind=kOutput, calls=%fused_computation.48.clone.1 | convolution fusion | flops 415629312 | bytes 14443520 | tf_op jit(solution)/shard_map/while/body/eval_jaxpr/hqk,qhd->khd/dot_general | solution.py:78
  472.4 3.0 copy.108
  475.9 1.6 copy.110
  477.8 1.6 copy.106
  479.9 1.6 copy.109
  481.8 3.9 fusion.126
  485.7 2.4 fusion.129
  490.7 3.0 copy.107
  493.7 1.6 copy.117
  495.6 8.1 %fusion.113 = f32[1024,768]{1,0:T(8,128)} fusion(bf16[768,2304]{1,0:T(8,128)(2,1)} %all-gather.7.cloned.1.call-done, bf16[1024,768]{0,1:T(8,128)(2,1)S(1)} %bitcast.200, bf16[1024,768]{0,1:T(8,128)(2,1)} %bitcast.210, bf16[1024,768]{0,1:T(8,128)(2,1)S(1)} %bitcast.203), kind=kOutput, calls=%fused_computation.102 | convolution fusion | flops 3638034432 | bytes 11403264 | tf_op jit(solution)/shard_map/dot_general | solution.py:224
  503.7 1.5 fusion.160
  505.2 41.6 %all-reduce.8.cloned.1.call-done = (f32[768,8]{0,1:T(8,128)}, f32[8,768]{1,0:T(8,128)}, f32[768,8]{0,1:T(8,128)}, f32[8,768]{1,0:T(8,128)}) async-done(((f32[768,8]{0,1:T(8,128)}, f32[8,768]{1,0:T(8,128)}, f32[768,8]{0,1:T(8,128)}, f32[8,768]{1,0:T(8,128)}), (f32[768,8]{0,1:T(8,128)}, f32[8,768]{1,0:T(8,128)}, f32[768,8]{0,1:T(8,128)}, f32[8,768]{1,0:T(8,128)})) %all-reduce.8.cloned.1.call-update) | async-done | bytes 98320 | tf_op jit(solution)/shard_map/psum | solution.py:15
  546.8 6.5 %add_add_fusion.2 = f32[1024,768]{1,0:T(8,128)} fusion(f32[1024,768]{1,0:T(8,128)S(1)} %fusion.160, f32[1024,768]{1,0:T(8,128)} %fusion.113, f32[1024,768]{1,0:T(8,128)} %copy-done.7, f32[1024,8]{0,1:T(8,128)S(1)} %convolution_multiply_fusion, bf16[768,8]{0,1:T(8,128)(2,1)S(1)} %copy-done.19, f32[1024]{0:T(1024)S(1)} %copy-done.24), kind=kOutput, calls=%fused_computation.125 | convolution fusion | flops 78643200 | bytes 12632064 | tf_op jit(solution)/shard_map/dot_general | solution.py:228
  553.3 49.6 %all-reduce.6.cloned.1.call-done = (f32[768,8]{0,1:T(8,128)}, f32[8,768]{1,0:T(8,128)}, f32[768,8]{0,1:T(8,128)}, f32[8,768]{1,0:T(8,128)}) async-done(((f32[768,8]{0,1:T(8,128)}, f32[8,768]{1,0:T(8,128)}, f32[768,8]{0,1:T(8,128)}, f32[8,768]{1,0:T(8,128)}), (f32[768,8]{0,1:T(8,128)}, f32[8,768]{1,0:T(8,128)}, f32[768,8]{0,1:T(8,128)}, f32[8,768]{1,0:T(8,128)})) %all-reduce.6.cloned.1.call-update) | async-done | bytes 98320 | tf_op jit(solution)/shard_map/psum | solution.py:15
  605.6 1.3 copy.158
  (134 shorter events, 23.7 us)
Async XLA Ops:
  7.2 179.3 %copy-start = (bf16[8,768]{1,0:T(8,128)(2,1)S(1)}, bf16[8,768]{1,0:T(8,128)(2,1)}, u32[]{:S(2)}) copy-start(bf16[8,768]{1,0:T(8,128)(2,1)} %param.43) | copy-start | bytes 36868
  7.2 169.8 %copy-start.1 = (bf16[2,512,768]{2,1,0:T(8,128)(2,1)S(1)}, bf16[2,512,768]{2,1,0:T(8,128)(2,1)}, u32[]{:S(2)}) copy-start(bf16[2,512,768]{2,1,0:T(8,128)(2,1)} %param.24) | copy-start | bytes 4718596
  7.2 66.4 %copy-start.32 = (bf16[96]{0:T(256)(128)(2,1)S(1)}, bf16[96]{0:T(256)(128)(2,1)}, u32[]{:S(2)}) copy-start(bf16[96]{0:T(256)(128)(2,1)} %param.36) | copy-start | bytes 580
  7.2 169.8 %all-gather.7.cloned.1.call-start = ((), (), s32[]{:S(2)}) async-start(), calls=%async_computation | async-start | bytes 3649536 | tf_op jit(solution)/shard_map/all_gather | solution.py:31
  7.9 234.0 %all-gather.9.cloned.1.call-start = ((), (), s32[]{:S(2)}) async-start(), calls=%async_computation.1 | async-start | bytes 1216512 | tf_op jit(solution)/shard_map/all_gather | solution.py:32
  8.7 239.4 %all-gather.11.cloned.1.call-start = ((), (), s32[]{:S(2)}) async-start(), calls=%async_computation.2 | async-start | bytes 4866048 | tf_op jit(solution)/shard_map/all_gather | solution.py:33
  9.4 275.3 %all-gather.13.cloned.1.call-start = ((), (), s32[]{:S(2)}) async-start(), calls=%async_computation.3 | async-start | bytes 4866048 | tf_op jit(solution)/shard_map/all_gather | solution.py:34
  10.0 536.8 %all-reduce.8.cloned.1.call-start = ((), (), s32[]{:S(2)}) async-start(), calls=%async_computation.5 | async-start | bytes 196608 | tf_op jit(solution)/shard_map/psum | solution.py:15
  71.6 111.4 %copy-start.14 = (f32[1024,8]{0,1:T(8,128)}, f32[1024,8]{0,1:T(8,128)S(1)}, u32[]{:S(2)}) copy-start(f32[1024,8]{0,1:T(8,128)S(1)} %fusion.158) | copy-start | bytes 98308
  73.5 122.9 %copy-start.12 = (f32[1024,8]{0,1:T(8,128)}, f32[1024,8]{0,1:T(8,128)S(1)}, u32[]{:S(2)}) copy-start(f32[1024,8]{0,1:T(8,128)S(1)} %fusion.159) | copy-start | bytes 98308
  182.9 3.6 copy-start.8
  191.2 5.3 copy-start.16
  217.1 3.8 copy-start.3
  228.5 3.8 copy-start.3
  237.4 4.6 copy-start.29
  245.9 1.7 copy-start.6
  245.9 2.2 copy-start.25
  245.9 2.2 copy-start.27
  245.9 2.2 copy-start.28
  248.2 36.6 %copy-start.26 = (f32[768]{0:T(1024)S(1)}, f32[768]{0:T(1024)}, u32[]{:S(2)}) copy-start(f32[768]{0:T(1024)} %get-tuple-element.175) | copy-start | bytes 9220
  284.8 16.1 %copy-start.9 = (bf16[2,512,768]{2,1,0:T(8,128)(2,1)S(1)}, bf16[2,512,768]{2,1,0:T(8,128)(2,1)}, u32[]{:S(2)}) copy-start(bf16[2,512,768]{2,1,0:T(8,128)(2,1)} %param.26) | copy-start | bytes 4718596
  284.8 16.1 %copy-start.20 = (f32[768]{0:T(1024)S(1)}, f32[768]{0:T(1024)}, u32[]{:S(2)}) copy-start(f32[768]{0:T(1024)} %get-tuple-element.182) | copy-start | bytes 9220
  300.8 1.1 copy-start.21
  300.8 1.1 copy-start.22
  302.0 3.3 copy-start.30
  328.3 5.3 copy-start.31
  331.9 1.8 copy-start.7
  331.9 1.7 copy-start.23
  345.8 6.4 %copy-start.4 = (bf16[2,512,12,64]{1,3,2,0:T(8,128)(2,1)S(1)}, bf16[2,512,12,64]{1,3,2,0:T(8,128)(2,1)}, u32[]{:S(2)}) copy-start(bf16[2,512,12,64]{1,3,2,0:T(8,128)(2,1)} %get-tuple-element.405) | copy-start | bytes 4718596 | tf_op jit(solution)/shard_map/while
  345.9 6.4 %copy-start.5 = (bf16[2,512,12,64]{1,3,2,0:T(8,128)(2,1)S(1)}, bf16[2,512,12,64]{1,3,2,0:T(8,128)(2,1)}, u32[]{:S(2)}) copy-start(bf16[2,512,12,64]{1,3,2,0:T(8,128)(2,1)} %get-tuple-element.404) | copy-start | bytes 4718596 | tf_op jit(solution)/shard_map/while
  409.0 6.4 %copy-start.4 = (bf16[2,512,12,64]{1,3,2,0:T(8,128)(2,1)S(1)}, bf16[2,512,12,64]{1,3,2,0:T(8,128)(2,1)}, u32[]{:S(2)}) copy-start(bf16[2,512,12,64]{1,3,2,0:T(8,128)(2,1)} %get-tuple-element.405) | copy-start | bytes 4718596 | tf_op jit(solution)/shard_map/while
  409.0 6.4 %copy-start.5 = (bf16[2,512,12,64]{1,3,2,0:T(8,128)(2,1)S(1)}, bf16[2,512,12,64]{1,3,2,0:T(8,128)(2,1)}, u32[]{:S(2)}) copy-start(bf16[2,512,12,64]{1,3,2,0:T(8,128)(2,1)} %get-tuple-element.404) | copy-start | bytes 4718596 | tf_op jit(solution)/shard_map/while
  475.9 1.9 copy-start.11
  479.4 2.0 copy-start.17
  479.8 1.9 copy-start.15
  479.8 5.8 copy-start.13
  481.4 4.3 copy-start.10
  481.4 6.6 %copy-start.2 = (bf16[2,512,768]{2,1,0:T(8,128)(2,1)S(1)}, bf16[2,512,768]{2,1,0:T(8,128)(2,1)}, u32[]{:S(2)}) copy-start(bf16[2,512,768]{2,1,0:T(8,128)(2,1)} %param.24) | copy-start | bytes 4718596
  495.4 107.5 %all-reduce.6.cloned.1.call-start = ((), (), s32[]{:S(2)}) async-start(), calls=%async_computation.4 | async-start | bytes 196608 | tf_op jit(solution)/shard_map/psum | solution.py:15
  495.6 8.1 %copy-start.18 = (bf16[768,8]{0,1:T(8,128)(2,1)S(1)}, bf16[768,8]{0,1:T(8,128)(2,1)}, u32[]{:S(2)}) copy-start(bf16[768,8]{0,1:T(8,128)(2,1)} %param.40) | copy-start | bytes 36868
  503.7 43.1 %copy-start.19 = (bf16[768,8]{0,1:T(8,128)(2,1)S(1)}, bf16[768,8]{0,1:T(8,128)(2,1)}, u32[]{:S(2)}) copy-start(bf16[768,8]{0,1:T(8,128)(2,1)} %param.42) | copy-start | bytes 36868
  503.7 43.1 %copy-start.24 = (f32[1024]{0:T(1024)S(1)}, f32[1024]{0:T(1024)}, u32[]{:S(2)}) copy-start(f32[1024]{0:T(1024)} %copy-done.23) | copy-start | bytes 12292
Sparse Core Ops, SparseCore 0:
  10.9 61.1 all-gather.6
  75.0 52.4 all-gather.8
  130.4 64.2 all-gather.10
  197.4 62.3 all-gather.12
  495.5 51.2 all-reduce.7
  549.4 53.4 all-reduce.5
